TPU v7x, 512 devices: a whole 4x4x16 slice. The times are simulated.
512 devices in a mesh: rows: 64 (over y, z), cols: 8 (over x, core).
Axes of the slice: x: 4, y: 4, z: 16, core: 2. Of those that a mesh axis runs over, the one named last changes fastest.
Arguments:
- images: float32 [512, 32, 128], P('rows'), may hold values from -6 to 6
- gauge_pixel: int32 [131072], P('rows'), may hold values from 0 to 32767
- row_mask: int32 [131072], P('rows'), may hold values 0 or 1
- gauge_counts: int32 [64], P('rows'), may hold values from 1 to 2048, as said below
- targets: float32 [131072], P('rows'), may hold values from -10 to 10
- theta: float32 [64, 8], replicated, may hold values from -2.5 to 2.5
- amplitude: float32 [64], replicated, may hold values from 0.5 to 1.5
- damping: float32 [], replicated, may hold values from 0.05 to 0.3
Outputs:
- r_factor: float32 [512, 512], replicated
- new_theta: float32 [64, 8], replicated
- predicted: float32 [131072], P(('rows', 'cols'))
Inputs may be any that keep to these rules, and one draw needn't show every extreme that they name: The slots in use on an index of rows are its first gauge_counts slots; one index of rows uses all 2048.
All inputs are finite; a program needn't handle non-finite values. No bound on the sum of `row_mask` on one device may be relied on, other than what follows from the above.
Results may differ from a plain program's by a relative error of at most 0.0003.
Values sent between devices are 32-bit elements; how exact they have to be, the bound alone decides.
A program may use at most 64 MiB of HBM per device.

v0:
```python
import jax
import jax.numpy as jnp
from jax import lax
from jax.sharding import PartitionSpec as P

BLOCK = 256
y_orders = [0, 1, 0, 2, 1, 0, 0, 0]
x_orders = [0, 0, 1, 0, 1, 2, 0, 2]
sigmas = [1.5, 1.5, 1.5, 1.5, 1.5, 1.5, 3.0, 3.0]


def kernel_values(spacing, deriv_order, width_sigma):
    envelope = jnp.exp(-spacing * spacing / (2.0 * width_sigma * width_sigma))
    if deriv_order == 1:
        return -spacing / width_sigma**2 * envelope
    if deriv_order == 2:
        return (spacing * spacing / width_sigma**4 - 1.0 / width_sigma**2) * envelope
    return envelope


def kernel_table(length, deriv_order, width_sigma):
    places = jnp.arange(length)
    spacing = (places[:, None] - places[None, :]).astype(jnp.float32)
    sample = jnp.arange(-12, 13).astype(jnp.float32)
    scaling = jnp.sqrt(jnp.sum(kernel_values(sample, deriv_order, width_sigma) ** 2))
    return kernel_values(spacing, deriv_order, width_sigma) / scaling


def features(clip_tiles):
    height = clip_tiles.shape[1]
    breadth = clip_tiles.shape[2]
    left_tabs = jnp.stack(
        [kernel_table(height, y_orders[which], sigmas[which]) for which in range(8)]
    )
    right_tabs = jnp.stack(
        [kernel_table(breadth, x_orders[which], sigmas[which]) for which in range(8)]
    )
    partial_conv = jnp.einsum(
        "kij,cjw->kciw", left_tabs, clip_tiles, precision=lax.Precision.HIGHEST
    )
    full_conv = jnp.einsum(
        "kciw,kvw->kciv", partial_conv, right_tabs, precision=lax.Precision.HIGHEST
    )
    return full_conv.reshape(full_conv.shape[0], -1)


def outer_rows(slope, phi):
    return (slope[:, :, None] * phi[:, None, :]).reshape(slope.shape[0], -1)


def solve_step(lower, rhs):
    inner = lax.linalg.triangular_solve(lower, rhs[:, None], left_side=True, lower=True)
    outer = lax.linalg.triangular_solve(lower, inner, left_side=True, lower=True, transpose_a=True)
    return -outer[:, 0]


def on_device(images, gauge_pixel, row_mask, gauge_counts, targets, theta, amplitude, damping):
    ncols = lax.axis_size("cols")
    column = lax.axis_index("cols")
    slots = gauge_pixel.shape[0]
    share = slots // ncols
    channels = theta.shape[0]
    basis_count = theta.shape[1]
    params = channels * basis_count
    local_width = channels // ncols
    own_params = local_width * basis_count
    count = gauge_counts[0]
    live = ((jnp.arange(slots) < count) & (row_mask == 1)).astype(jnp.float32)
    flat_feats = features(images)
    phi = jnp.take(flat_feats, gauge_pixel, axis=1).T
    act = jnp.tanh(jnp.dot(phi, theta.T, precision=lax.Precision.HIGHEST))
    model = jnp.dot(act, amplitude, precision=lax.Precision.HIGHEST)
    resid = live * (model - targets)
    slope = live[:, None] * amplitude[None, :] * (1.0 - act * act)

    def block_rows(values):
        return lax.dynamic_slice_in_dim(values, column * share, share, 0)

    def pick(values):
        return block_rows(values)

    local_slope = lax.dynamic_slice_in_dim(slope, column * local_width, local_width, 1)
    jac_cols = outer_rows(local_slope, phi)
    prefix = jnp.clip(count - column * share, 0, share)
    assigned = lax.all_to_all(jac_cols, "cols", split_axis=0, concat_axis=1, tiled=True)
    assigned_resid = pick(resid)
    trips = (prefix + BLOCK - 1) // BLOCK

    def add_block(which, carry):
        gram = carry[0] + lax.dot_general(
            assigned,
            assigned,
            (((0,), (0,)), ((), ())),
            precision=lax.Precision.HIGHEST,
            preferred_element_type=jnp.float32,
        )
        grad = carry[1] + jnp.dot(assigned_resid, assigned, precision=lax.Precision.HIGHEST)
        return (gram, grad)

    start = (jnp.zeros((params, params), jnp.float32), jnp.zeros((params,), jnp.float32))
    gram_part, grad_part = lax.fori_loop(0, trips, add_block, start)
    live_part = jnp.sum(pick(live))
    gram, grad, total = lax.psum((gram_part, grad_part, live_part), ("rows", "cols"))
    normal = gram / total + damping * jnp.eye(params, dtype=jnp.float32)
    lower = jnp.linalg.cholesky(normal)
    step = solve_step(lower, grad / total)
    local_step = lax.dynamic_slice_in_dim(step, column * own_params, own_params, 0)
    linear_part = lax.psum_scatter(
        jnp.dot(jac_cols, local_step, precision=lax.Precision.HIGHEST),
        "cols",
        scatter_dimension=0,
        tiled=True,
    )
    predicted = block_rows(resid) + linear_part
    return (lower.T, theta + step.reshape(channels, basis_count), predicted)


def solution(mesh):
    return jax.shard_map(
        on_device,
        mesh=mesh,
        in_specs=(P("rows", None, None), P("rows"), P("rows"), P("rows"), P("rows"), P(), P(), P()),
        out_specs=(P(), P(), P(("rows", "cols"))),
        check_vma=False,
    )
```

profile of v0, /device:TPU:8, one launch (start us, length us, event | category | flops | bytes accessed | tf_op | source)
XLA Modules:
  0.0 705.4 jit_solution(6471413244750945603)
XLA Ops:
  16.3 1.0 convolution_bitcast_fusion
  17.3 1.1 fusion.15
  18.4 8.6 %copy.61 = f32[8,8,32,128]{0,3,2,1:T(8,128)} copy(f32[8,8,32,128]{3,2,1,0:T(8,128)S(1)} %fusion.15) | data formatting | bytes 2097152 | tf_op jit(solution)/shard_map/reshape | solution.py:44
  27.0 11.2 %gather_fusion = f32[2048,8]{1,0:T(8,128)S(1)} fusion(f32[8,32768]{0,1:T(8,128)} %bitcast.185, s32[2048]{0:T(1024)S(1)} %fusion.50), kind=kCustom, calls=%fused_computation | custom fusion | bytes 139264 | tf_op jit(solution)/shard_map/jit(_take)/gather | solution.py:70
  38.8 1.3 convolution_tanh_fusion
  40.6 1.0 copy.43
  41.5 4.3 all-to-all-start
  46.3 0.8 dynamic-slice_select_fusion
  47.1 9.1 %all-to-all-done = f32[8,256,64]{1,2,0:T(8,128)S(1)} async-done(((f32[8,256,64]{1,2,0:T(8,128)}), f32[8,256,64]{1,2,0:T(8,128)S(1)}, u32[]{:S(2)}, u32[]{:S(2)}) %all-to-all-start) | async-done | bytes 524320 | tf_op jit(solution)/shard_map/all_to_all | solution.py:85
  56.1 1.0 fusion.83
  58.2 1.3 copy.45
  60.9 1.3 dynamic-slice.4
  62.9 108.7 %all-reduce.2 = (f32[]{:T(128)}, f32[512]{0:T(512)S(1)}) all-reduce(f32[]{:T(128)} %dynamic-slice_reduce_fusion, f32[512]{0:T(512)S(1)} %get-tuple-element.82), channel_id=1, replica_groups=mesh['rows'=64,'cols'=8] {'rows','cols'}, use_global_device_ids=true, to_apply=%region_9.0 | all-reduce | flops 513 | bytes 4104 | tf_op jit(solution)/shard_map/psum | solution.py:103
  172.3 363.3 %all-reduce.5.cloned.1.call-done = f32[512,512]{0,1:T(8,128)} async-done(((f32[512,512]{0,1:T(8,128)}), f32[512,512]{0,1:T(8,128)}) %all-reduce.5.cloned.1.call-update) | async-done | bytes 1048592 | tf_op jit(solution)/shard_map/psum | solution.py:103
  535.6 2.0 select_add_fusion
  537.9 2.1 fusion.12
  540.1 11.7 %cholesky.103 = f32[128,128]{1,0:T(8,128)S(1)} custom-call(f32[128,128]{1,0:T(8,128)S(1)} %cholesky.263), custom_call_target="Cholesky" | custom-call | tf_op jit(solution)/shard_map/jit(cholesky)/cholesky | solution.py:105
  551.8 9.8 %custom-call.32 = f32[1,128,128]{1,2,0:T(8,128)S(1)} custom-call(f32[1,128,128]{2,1,0:T(8,128)S(1)} %get-tuple-element.162), custom_call_target="InvertDiagBlocksLowerTriangular" | custom-call | tf_op jit(solution)/shard_map/jit(cholesky)/cholesky | solution.py:105
  562.3 11.7 %cholesky.215 = f32[128,128]{1,0:T(8,128)S(1)} custom-call(f32[128,128]{1,0:T(8,128)S(1)} %cholesky.267), custom_call_target="Cholesky" | custom-call | tf_op jit(solution)/shard_map/jit(cholesky)/cholesky | solution.py:105
  574.5 9.9 %custom-call.33 = f32[1,128,128]{1,2,0:T(8,128)S(1)} custom-call(f32[1,128,128]{2,1,0:T(8,128)S(1)} %get-tuple-element.160), custom_call_target="InvertDiagBlocksLowerTriangular" | custom-call | tf_op jit(solution)/shard_map/jit(cholesky)/cholesky | solution.py:105
  585.5 11.7 %cholesky.236 = f32[128,128]{1,0:T(8,128)S(1)} custom-call(f32[128,128]{1,0:T(8,128)S(1)} %cholesky.272), custom_call_target="Cholesky" | custom-call | tf_op jit(solution)/shard_map/jit(cholesky)/cholesky | solution.py:105
  597.3 9.8 %custom-call.34 = f32[1,128,128]{1,2,0:T(8,128)S(1)} custom-call(f32[1,128,128]{2,1,0:T(8,128)S(1)} %get-tuple-element.158), custom_call_target="InvertDiagBlocksLowerTriangular" | custom-call | tf_op jit(solution)/shard_map/jit(cholesky)/cholesky | solution.py:105
  607.9 11.9 %cholesky.253 = f32[128,128]{1,0:T(8,128)S(1)} custom-call(f32[128,128]{1,0:T(8,128)S(1)} %convolution_subtract_fusion.2), custom_call_target="Cholesky" | custom-call | tf_op jit(solution)/shard_map/jit(cholesky)/cholesky | solution.py:105
  620.0 0.7 compare_reduce_fusion.1
  624.5 1.2 fusion.13
  625.8 11.3 %while.16 = (s32[]{:T(128)}, f32[512,512]{0,1:T(8,128)S(1)}, s32[4,2]{0,1:T(2,128)S(1)}, f32[4,128,128]{2,1,0:T(8,128)}, s32[]{:T(128)}) while((s32[]{:T(128)}, f32[512,512]{0,1:T(8,128)S(1)}, s32[4,2]{0,1:T(2,128)S(1)}, f32[4,128,128]{2,1,0:T(8,128)}, s32[]{:T(128)}) %tuple.61), condition=%wide.while_cond, body=%wide.while_body.sunk | while | flops 2 | bytes 393829 | solution.py:53
  626.4 1.4 dynamic-slice.12
  629.3 1.4 dynamic-slice.12
  632.1 1.4 dynamic-slice.12
  634.9 1.4 dynamic-slice.12
  637.1 40.1 %custom-call.35 = f32[4,128,128]{1,2,0:T(8,128)S(1)} custom-call(f32[4,128,128]{2,1,0:T(8,128)} %get-tuple-element.90), custom_call_target="InvertDiagBlocksLowerTriangular" | custom-call | tf_op jit(solution)/shard_map/triangular_solve | solution.py:53
  681.7 15.2 %all-reduce.1 = f32[2048]{0:T(1024)S(1)} all-reduce(f32[2048]{0:T(1024)S(1)} %bitcast.197), channel_id=2, replica_groups=mesh['rows'=64,'cols'=8] {'cols'}, use_global_device_ids=true, to_apply=%region_19.20.clone | all-reduce | flops 2048 | bytes 16384
  (116 shorter events, 25.3 us)
Async XLA Ops:
  7.2 9.1 %copy-start = (f32[8,32,128]{2,1,0:T(8,128)S(1)}, f32[8,32,128]{2,1,0:T(8,128)}, u32[]{:S(2)}) copy-start(f32[8,32,128]{2,1,0:T(8,128)} %param.10) | copy-start | bytes 393220
  7.2 31.7 %copy-start.1 = (f32[64,8]{0,1:T(8,128)S(1)}, f32[64,8]{0,1:T(8,128)}, u32[]{:S(2)}) copy-start(f32[64,8]{0,1:T(8,128)} %param.15) | copy-start | bytes 6148
  7.2 33.0 %copy-start.3 = (f32[64]{0:T(128)S(1)}, f32[64]{0:T(128)}, u32[]{:S(2)}) copy-start(f32[64]{0:T(128)} %param.16) | copy-start | bytes 772
  7.2 33.1 %copy-start.2 = (s32[2048]{0:T(1024)S(1)}, s32[2048]{0:T(1024)}, u32[]{:S(2)}) copy-start(s32[2048]{0:T(1024)} %param.12) | copy-start | bytes 24580
  41.5 14.6 %all-to-all-start = ((f32[8,256,64]{1,2,0:T(8,128)}), f32[8,256,64]{1,2,0:T(8,128)S(1)}, u32[]{:S(2)}, u32[]{:S(2)}) async-start(f32[8,256,64]{1,2,0:T(8,128)} %copy.43), calls=%async_computation | async-start | bytes 1048576 | tf_op jit(solution)/shard_map/all_to_all | solution.py:85
  45.8 489.8 %all-reduce.5.cloned.1.call-start = ((), (), s32[]{:S(2)}) async-start(), calls=%async_computation.1 | async-start | bytes 2097152 | tf_op jit(solution)/shard_map/psum | solution.py:103
Sparse Core Ops, SparseCore 0:
  59.6 475.9 all-reduce.4
where the time goes:
time: 712 us; the launch traced here: 705 us
  waiting for transfers between devices  372 us (52%)
  other arithmetic  133 us (19%)
  blocking collectives  124 us (17%)
  local copies, waits for them, and re-layouts  37.7 us (5%)
  between operations  22.7 us (3%)
  matrix products  10.9 us (2%)
    psum x1, waiting for transfers between devices, on_device(): lax.psum((gram_part, grad_part, live_part), ('rows', 'cols'))  363 us
    psum x1, blocking collectives, on_device(): lax.psum((gram_part, grad_part, live_part), ('rows', 'cols'))  109 us
    another operation x14, other arithmetic, on_device(): lower = jnp.linalg.cholesky(normal)  78.7 us
    another operation x3, other arithmetic, solve_step(): lax.linalg.triangular_solve(lower, inner, left_side=True, lower=True, tra...  41.4 us
    unnamed x1, blocking collectives  15.2 us
  transfers between devices with their start and end apart: 2, of which 2 were waited for; matrix products, arithmetic and copies ran while one was open for 1% of the time, Pallas kernels for 0%

commit v1 on v0

--- a/solution.py
+++ b/solution.py
@@ -100,7 +100,7 @@
     start = (jnp.zeros((params, params), jnp.float32), jnp.zeros((params,), jnp.float32))
     gram_part, grad_part = lax.fori_loop(0, trips, add_block, start)
     live_part = jnp.sum(pick(live))
-    gram, grad, total = lax.psum((gram_part, grad_part, live_part), ("rows", "cols"))
+    gram, grad, total = lax.psum(lax.psum((gram_part, grad_part, live_part), "cols"), "rows")
     normal = gram / total + damping * jnp.eye(params, dtype=jnp.float32)
     lower = jnp.linalg.cholesky(normal)
     step = solve_step(lower, grad / total)

time: 712 us -> 594 us (0.83)
  the two profiles are of different devices: /device:TPU:8 before, /device:TPU:1 now
where the time goes in v1:
time: 594 us; the launch traced here: 587 us
  waiting for transfers between devices  218 us (37%)
  blocking collectives  154 us (26%)
  other arithmetic  133 us (22%)
  local copies, waits for them, and re-layouts  37.7 us (6%)
  between operations  22.7 us (4%)
  matrix products  10.9 us (2%)
  starting transfers between devices  10.3 us (2%)
    psum x1, waiting for transfers between devices, on_device(): lax.psum(lax.psum((gram_part, grad_part, live_part), 'cols'), 'rows')  135 us
    psum x1, blocking collectives, on_device(): lax.psum(lax.psum((gram_part, grad_part, live_part), 'cols'), 'rows')  117 us
    another operation x14, other arithmetic, on_device(): lower = jnp.linalg.cholesky(normal)  78.7 us
    psum x1, waiting for transfers between devices, on_device(): lax.psum((gram_part, grad_part, live_part), 'cols')  74.9 us
    another operation x3, other arithmetic, solve_step(): lax.linalg.triangular_solve(lower, inner, left_side=True, lower=True, tra...  41.4 us
    unnamed x1, blocking collectives  22.7 us
    psum x1, blocking collectives, on_device(): lax.psum((gram_part, grad_part, live_part), 'cols')  14.6 us
  transfers between devices with their start and end apart: 3, of which 3 were waited for; matrix products, arithmetic and copies ran while one was open for 1% of the time, Pallas kernels for 0%

profile of v1, /device:TPU:1, one launch (start us, length us, event | category | flops | bytes accessed | tf_op | source)
XLA Modules:
  0.0 587.3 jit_solution(17321946728605778132)
XLA Ops:
  16.3 1.0 convolution_bitcast_fusion
  17.3 1.1 fusion.15
  18.4 8.6 %copy.61 = f32[8,8,32,128]{0,3,2,1:T(8,128)} copy(f32[8,8,32,128]{3,2,1,0:T(8,128)S(1)} %fusion.15) | data formatting | bytes 2097152 | tf_op jit(solution)/shard_map/reshape | solution.py:44
  27.0 11.2 %gather_fusion = f32[2048,8]{1,0:T(8,128)S(1)} fusion(f32[8,32768]{0,1:T(8,128)} %bitcast.185, s32[2048]{0:T(1024)S(1)} %fusion.50), kind=kCustom, calls=%fused_computation | custom fusion | bytes 139264 | tf_op jit(solution)/shard_map/jit(_take)/gather | solution.py:70
  38.8 1.3 convolution_tanh_fusion
  40.6 1.0 copy.43
  41.5 10.2 %all-to-all-start = ((f32[8,256,64]{1,2,0:T(8,128)}), f32[8,256,64]{1,2,0:T(8,128)S(1)}, u32[]{:S(2)}, u32[]{:S(2)}) async-start(f32[8,256,64]{1,2,0:T(8,128)} %copy.43), calls=%async_computation | async-start | bytes 1048576 | tf_op jit(solution)/shard_map/all_to_all | solution.py:85
  52.9 8.2 %all-to-all-done = f32[8,256,64]{1,2,0:T(8,128)S(1)} async-done(((f32[8,256,64]{1,2,0:T(8,128)}), f32[8,256,64]{1,2,0:T(8,128)S(1)}, u32[]{:S(2)}, u32[]{:S(2)}) %all-to-all-start) | async-done | bytes 524320 | tf_op jit(solution)/shard_map/all_to_all | solution.py:85
  61.1 1.0 fusion.83
  63.2 1.3 copy.45
  64.6 74.9 %all-reduce.7.cloned.1.call-done = f32[512,512]{0,1:T(8,128)} async-done(((f32[512,512]{0,1:T(8,128)}), f32[512,512]{0,1:T(8,128)}) %all-reduce.7.cloned.1.call-update) | async-done | bytes 1048592 | tf_op jit(solution)/shard_map/psum | solution.py:103
  140.9 1.3 dynamic-slice.4
  142.8 14.6 %all-reduce.3 = (f32[]{:T(128)}, f32[512]{0:T(512)S(1)}) all-reduce(f32[]{:T(128)} %dynamic-slice_reduce_fusion, f32[512]{0:T(512)S(1)} %get-tuple-element.82), channel_id=1, replica_groups=mesh['rows'=64,'cols'=8] {'cols'}, use_global_device_ids=true, to_apply=%region_10.0 | all-reduce | flops 513 | bytes 4104 | tf_op jit(solution)/shard_map/psum | solution.py:103
  157.4 117.2 %all-reduce.2 = (f32[]{:T(128)}, f32[512]{0:T(512)S(1)}) all-reduce(f32[]{:T(128)} %get-tuple-element.149, f32[512]{0:T(512)S(1)} %get-tuple-element.150), channel_id=1, replica_groups=mesh['rows'=64,'cols'=8] {'rows'}, use_global_device_ids=true, to_apply=%region_11.0 | all-reduce | flops 513 | bytes 4104 | tf_op jit(solution)/shard_map/psum | solution.py:103
  275.3 134.7 %all-reduce.9.cloned.1.call-done = f32[512,512]{0,1:T(8,128)} async-done(((f32[512,512]{0,1:T(8,128)}), f32[512,512]{0,1:T(8,128)}) %all-reduce.9.cloned.1.call-update) | async-done | bytes 1048592 | tf_op jit(solution)/shard_map/psum | solution.py:103
  410.0 2.0 select_add_fusion
  412.3 2.1 fusion.12
  414.5 11.7 %cholesky.103 = f32[128,128]{1,0:T(8,128)S(1)} custom-call(f32[128,128]{1,0:T(8,128)S(1)} %cholesky.263), custom_call_target="Cholesky" | custom-call | tf_op jit(solution)/shard_map/jit(cholesky)/cholesky | solution.py:105
  426.2 9.8 %custom-call.32 = f32[1,128,128]{1,2,0:T(8,128)S(1)} custom-call(f32[1,128,128]{2,1,0:T(8,128)S(1)} %get-tuple-element.164), custom_call_target="InvertDiagBlocksLowerTriangular" | custom-call | tf_op jit(solution)/shard_map/jit(cholesky)/cholesky | solution.py:105
  436.7 11.7 %cholesky.215 = f32[128,128]{1,0:T(8,128)S(1)} custom-call(f32[128,128]{1,0:T(8,128)S(1)} %cholesky.267), custom_call_target="Cholesky" | custom-call | tf_op jit(solution)/shard_map/jit(cholesky)/cholesky | solution.py:105
  448.9 9.9 %custom-call.33 = f32[1,128,128]{1,2,0:T(8,128)S(1)} custom-call(f32[1,128,128]{2,1,0:T(8,128)S(1)} %get-tuple-element.162), custom_call_target="InvertDiagBlocksLowerTriangular" | custom-call | tf_op jit(solution)/shard_map/jit(cholesky)/cholesky | solution.py:105
  459.9 11.7 %cholesky.236 = f32[128,128]{1,0:T(8,128)S(1)} custom-call(f32[128,128]{1,0:T(8,128)S(1)} %cholesky.272), custom_call_target="Cholesky" | custom-call | tf_op jit(solution)/shard_map/jit(cholesky)/cholesky | solution.py:105
  471.7 9.8 %custom-call.34 = f32[1,128,128]{1,2,0:T(8,128)S(1)} custom-call(f32[1,128,128]{2,1,0:T(8,128)S(1)} %get-tuple-element.160), custom_call_target="InvertDiagBlocksLowerTriangular" | custom-call | tf_op jit(solution)/shard_map/jit(cholesky)/cholesky | solution.py:105
  482.3 11.9 %cholesky.253 = f32[128,128]{1,0:T(8,128)S(1)} custom-call(f32[128,128]{1,0:T(8,128)S(1)} %convolution_subtract_fusion.2), custom_call_target="Cholesky" | custom-call | tf_op jit(solution)/shard_map/jit(cholesky)/cholesky | solution.py:105
  498.9 1.2 fusion.13
  500.1 11.3 %while.16 = (s32[]{:T(128)}, f32[512,512]{0,1:T(8,128)S(1)}, s32[4,2]{0,1:T(2,128)S(1)}, f32[4,128,128]{2,1,0:T(8,128)}, s32[]{:T(128)}) while((s32[]{:T(128)}, f32[512,512]{0,1:T(8,128)S(1)}, s32[4,2]{0,1:T(2,128)S(1)}, f32[4,128,128]{2,1,0:T(8,128)}, s32[]{:T(128)}) %tuple.61), condition=%wide.while_cond, body=%wide.while_body.sunk | while | flops 2 | bytes 393829 | solution.py:53
  500.8 1.4 dynamic-slice.12
  503.6 1.4 dynamic-slice.12
  506.5 1.4 dynamic-slice.12
  509.3 1.4 dynamic-slice.12
  511.4 40.1 %custom-call.35 = f32[4,128,128]{1,2,0:T(8,128)S(1)} custom-call(f32[4,128,128]{2,1,0:T(8,128)} %get-tuple-element.90), custom_call_target="InvertDiagBlocksLowerTriangular" | custom-call | tf_op jit(solution)/shard_map/triangular_solve | solution.py:53
  556.1 22.7 %all-reduce.1 = f32[2048]{0:T(1024)S(1)} all-reduce(f32[2048]{0:T(1024)S(1)} %bitcast.197), channel_id=2, replica_groups=mesh['rows'=64,'cols'=8] {'cols'}, use_global_device_ids=true, to_apply=%region_22.23.clone | all-reduce | flops 2048 | bytes 16384
  (120 shorter events, 26.8 us)
Async XLA Ops:
  7.2 9.1 %copy-start = (f32[8,32,128]{2,1,0:T(8,128)S(1)}, f32[8,32,128]{2,1,0:T(8,128)}, u32[]{:S(2)}) copy-start(f32[8,32,128]{2,1,0:T(8,128)} %param.10) | copy-start | bytes 393220
  7.2 31.7 %copy-start.1 = (f32[64,8]{0,1:T(8,128)S(1)}, f32[64,8]{0,1:T(8,128)}, u32[]{:S(2)}) copy-start(f32[64,8]{0,1:T(8,128)} %param.15) | copy-start | bytes 6148
  7.2 33.0 %copy-start.3 = (f32[64]{0:T(128)S(1)}, f32[64]{0:T(128)}, u32[]{:S(2)}) copy-start(f32[64]{0:T(128)} %param.16) | copy-start | bytes 772
  7.2 33.1 %copy-start.2 = (s32[2048]{0:T(1024)S(1)}, s32[2048]{0:T(1024)}, u32[]{:S(2)}) copy-start(s32[2048]{0:T(1024)} %param.12) | copy-start | bytes 24580
  41.5 19.6 %all-to-all-start = ((f32[8,256,64]{1,2,0:T(8,128)}), f32[8,256,64]{1,2,0:T(8,128)S(1)}, u32[]{:S(2)}, u32[]{:S(2)}) async-start(f32[8,256,64]{1,2,0:T(8,128)} %copy.43), calls=%async_computation | async-start | bytes 1048576 | tf_op jit(solution)/shard_map/all_to_all | solution.py:85
  51.8 87.7 %all-reduce.7.cloned.1.call-start = ((), (), s32[]{:S(2)}) async-start(), calls=%async_computation.1 | async-start | bytes 2097152 | tf_op jit(solution)/shard_map/psum | solution.py:103
  64.5 345.5 %all-reduce.9.cloned.1.call-start = ((), (), s32[]{:S(2)}) async-start(), calls=%async_computation.2 | async-start | bytes 2097152 | tf_op jit(solution)/shard_map/psum | solution.py:103
Sparse Core Ops, SparseCore 0:
  64.6 74.7 all-reduce.6
  142.8 267.1 all-reduce.8
